TPU v7x, 32 devices: a whole 2x2x4 slice. The times are simulated.
32 devices in a mesh: segment: 2 (over y), frame: 16 (over z, x, core).
Axes of the slice: x: 2, y: 2, z: 4, core: 2. Of those that a mesh axis runs over, the one named last changes fastest.
Arguments:
- noisy_clips: bfloat16 [4, 16, 16, 16, 512], P(None, 'frame'), may hold values from -6 to 6
- conv_first: bfloat16 [2, 9, 512, 512], P('segment', None, 'frame'), may hold values from -0.09375 to 0.09375
- conv_second: bfloat16 [2, 9, 512, 512], P('segment', None, 'frame'), may hold values from -0.09375 to 0.09375
- temporal: bfloat16 [2, 3, 512, 512], P('segment', None, 'frame'), may hold values from -0.15625 to 0.15625
Outputs:
- denoised: bfloat16 [4, 16, 16, 16, 512], P(None, 'frame', 'segment')
All inputs are finite; a program needn't handle non-finite values.
Results may differ from a plain program's by a relative error of at most 0.013.
Values may be sent and summed in bfloat16 or wider, within the bound.
A program may use at most 64 MiB of HBM per device.

v0:
```python
import jax
import jax.numpy as jnp
from jax import lax
from jax.sharding import PartitionSpec as P

skip_scale = 0.7071067811865476


def passed_along(shard, axis, by):
    length = lax.axis_size(axis)
    pairs = [(i, i + by) for i in range(length) if 0 <= i + by < length]
    return lax.ppermute(shard, axis, pairs)


def extended_2(cells, sides, width):
    for axis, dim in sides:
        count = lax.axis_size(axis)
        ends = count - 1
        head = lax.slice_in_dim(cells, 0, width, axis=dim)
        tail = lax.slice_in_dim(cells, cells.shape[dim] - width, cells.shape[dim], axis=dim)
        cells = jnp.concatenate(
            [
                lax.ppermute(tail, axis, [(i, (i + 1) % count) for i in range(ends)]),
                cells,
                lax.ppermute(head, axis, [((i + 1) % count, i) for i in range(ends)]),
            ],
            axis=dim,
        )
    return cells


def broadcast(shard, axis, root):
    mine = lax.axis_index(axis) == root
    return lax.psum(jnp.where(mine, shard, jnp.zeros_like(shard)), axis)


def spatial(field_in, kernel):
    extent = field_in.shape[1]
    channels = field_in.shape[3]
    padded = jnp.pad(field_in, ((0, 0), (1, 1), (1, 1), (0, 0)))
    accumulated = jnp.zeros((field_in.shape[0] * extent * extent, channels), jnp.float32)
    for row_shift in range(3):
        for col_shift in range(3):
            window = padded[
                :, row_shift : row_shift + extent, col_shift : col_shift + extent, :
            ].reshape(-1, channels)
            accumulated = accumulated + jnp.dot(
                window, kernel[3 * row_shift + col_shift], preferred_element_type=jnp.float32
            )
    return accumulated.reshape(field_in.shape)


def temporal_mix(extended, kernel, frame_local):
    channels = extended.shape[3]
    out_shape = (frame_local,) + extended.shape[1:]
    accumulated = jnp.zeros(out_shape, jnp.float32)
    for offset in range(3):
        window = extended[offset : offset + frame_local].reshape(-1, channels)
        accumulated = accumulated + jnp.dot(
            window, kernel[offset], preferred_element_type=jnp.float32
        ).reshape(out_shape)
    return accumulated


def on_device(noisy_clips, conv_first, conv_second, temporal):
    sections = lax.axis_size("segment")
    segment_id = lax.axis_index("segment")
    first_full, second_full, time_full = (
        lax.all_gather(conv_first, "frame", axis=2, tiled=True),
        lax.all_gather(conv_second, "frame", axis=2, tiled=True),
        lax.all_gather(temporal, "frame", axis=2, tiled=True),
    )
    first_kernel = first_full[0]
    second_kernel = second_full[0]
    time_kernel = time_full[0]
    clip_count = noisy_clips.shape[0]
    frame_local = noisy_clips.shape[1]
    side_len = noisy_clips.shape[2]
    block_shape = noisy_clips.shape[1:]
    tick_count = clip_count + sections - 1
    half_sections = sections // 2
    is_up = segment_id >= half_sections
    store_depth = max(half_sections - 1, 1)
    side_store = jnp.zeros((store_depth,) + block_shape, jnp.bfloat16)
    out_store = jnp.zeros(noisy_clips.shape, jnp.bfloat16)
    prev_out = jnp.zeros(block_shape, jnp.bfloat16)

    def tick_step(carry, tick_index):
        prev_out, side_store, out_store = carry
        clip_now = tick_index - segment_id
        active = (clip_now >= 0) & (clip_now < clip_count)
        clip_slot = jnp.clip(clip_now, 0, clip_count - 1)
        own_input = lax.dynamic_index_in_dim(noisy_clips, clip_slot, 0, keepdims=False)
        received, side_store = passed_along((prev_out, side_store), "segment", 1)
        entering = jnp.where(segment_id == 0, own_input, received)
        written = (jnp.arange(store_depth) == segment_id - 1) & (segment_id < half_sections)
        side_store = jnp.where(written[:, None, None, None, None], entering[None], side_store)
        stack_slot = jnp.clip(sections - 2 - segment_id, 0, store_depth - 1)
        stored = lax.dynamic_index_in_dim(side_store, stack_slot, 0, keepdims=False)
        skip_feature = jnp.where(segment_id == sections - 1, own_input, stored)
        joined = (
            (entering.astype(jnp.float32) + skip_feature.astype(jnp.float32)) * skip_scale
        ).astype(jnp.bfloat16)
        section_in = jnp.where(is_up, joined, entering)
        activated = lax.cond(
            active,
            lambda: jax.nn.silu(spatial(section_in, first_kernel)).astype(jnp.bfloat16),
            lambda: jnp.zeros(block_shape, jnp.bfloat16),
        )
        extended = extended_2(activated, (("frame", 0),), 1)

        def second_pass():
            branch_sum = spatial(activated, second_kernel) + temporal_mix(
                extended, time_kernel, frame_local
            )
            return (section_in.astype(jnp.float32) + jax.nn.silu(branch_sum)).astype(jnp.bfloat16)

        section_out = lax.cond(active, second_pass, lambda: jnp.zeros(block_shape, jnp.bfloat16))
        finished = (jnp.arange(clip_count) == clip_slot) & active & (segment_id == sections - 1)
        out_store = jnp.where(finished[:, None, None, None, None], section_out[None], out_store)
        return ((section_out, side_store, out_store), None)

    final_carry, unused = lax.scan(
        tick_step, (prev_out, side_store, out_store), jnp.arange(tick_count, dtype=jnp.int32)
    )
    delivered = broadcast(final_carry[2], "segment", sections - 1)
    slab_rows = side_len // sections
    return lax.dynamic_slice_in_dim(delivered, segment_id * slab_rows, slab_rows, 2)


def solution(mesh):
    in_specs = (
        P(None, "frame", None, None, None),
        P("segment", None, "frame", None),
        P("segment", None, "frame", None),
        P("segment", None, "frame", None),
    )
    out_specs = P(None, "frame", "segment", None, None)
    return jax.shard_map(
        on_device, mesh=mesh, in_specs=in_specs, out_specs=out_specs, check_vma=False
    )
```

profile of v0, /device:TPU:0, one launch (start us, length us, event | category | flops | bytes accessed | tf_op | source)
XLA Modules:
  0.0 428.6 jit_solution(14071804297938684224)
XLA Ops:
  8.8 43.1 %all-gather.8.cloned.1.call-done = bf16[1,3,512,512]{3,2,1,0:T(8,128)(2,1)} async-done(((bf16[1,3,32,512]{3,2,1,0:T(8,128)(2,1)}), bf16[1,3,512,512]{3,2,1,0:T(8,128)(2,1)}) %all-gather.8.cloned.1.call-update) | async-done | bytes 1572880 | tf_op jit(solution)/shard_map/all_gather | solution.py:71
  51.9 53.9 %all-gather.4.cloned.1.call-done = bf16[1,9,512,512]{3,2,1,0:T(8,128)(2,1)} async-done(((bf16[1,9,32,512]{3,2,1,0:T(8,128)(2,1)}), bf16[1,9,512,512]{3,2,1,0:T(8,128)(2,1)}) %all-gather.4.cloned.1.call-update) | async-done | bytes 4718608 | tf_op jit(solution)/shard_map/all_gather | solution.py:69
  105.8 53.7 %all-gather.6.cloned.1.call-done = bf16[1,9,512,512]{3,2,1,0:T(8,128)(2,1)} async-done(((bf16[1,9,32,512]{3,2,1,0:T(8,128)(2,1)}), bf16[1,9,512,512]{3,2,1,0:T(8,128)(2,1)}) %all-gather.6.cloned.1.call-update) | async-done | bytes 4718608 | tf_op jit(solution)/shard_map/all_gather | solution.py:70
  160.3 192.8 %while.17 = (s32[]{:T(128)}, bf16[1,16,16,512]{3,2,1,0:T(8,128)(2,1)}, bf16[1,1,16,16,512]{4,3,2,1,0:T(8,128)(2,1)}, bf16[4,1,16,16,512]{4,3,2,1,0:T(8,128)(2,1)...) while((s32[]{:T(128)}, ...), condition=%wide.region_5.6_spmd.clone, body=%wide.region_0.5_spmd.clone.sunk | while | flops 2824994816 | bytes 95421016 | solution.py:123
  160.3 3.4 collective-permute-start.1
  166.4 4.0 collective-permute-done.1
  170.3 5.0 %collective-permute-done = bf16[1,16,16,512]{3,2,1,0:T(8,128)(2,1)S(1)} collective-permute-done((bf16[1,16,16,512]{3,2,1,0:T(8,128)(2,1)}, bf16[1,16,16,512]{3,2,1,0:T(8,128)(2,1)S(1)}, u32[]{:S(2)}, u32[]{:S(2)}) %collective-permute-start) | collective-permute-done | bytes 262176 | tf_op jit(solution)/shard_map/while/body/eval_jaxpr/ppermute | solution.py:12
  177.3 5.4 %conditional.6 = (bf16[1,16,16,512]{3,2,1,0:T(8,128)(2,1)S(1)}) conditional(s32[]{:T(128)} %convert_element_type.72, () %tuple.67, (bf16[1,16,16,512]{3,2,1,0:T(8,128)(2,1)S(1)}, bf16[9,512,512]{2,1,0:T(8,128)(2,1)}) %tuple.68), branch_computations={%region_1.1_spmd, %region_2.2_spmd} | conditional | flops 1209663488 | bytes 38010916 | solution.py:105
  185.4 3.0 collective-permute-done.3
  188.4 8.0 %conditional.7 = (bf16[1,16,16,512]{3,2,1,0:T(8,128)(2,1)}) conditional(s32[]{:T(128)} %convert_element_type.72, () %tuple.66, (bf16[1,16,16,512]{3,2,1,0:T(8,128)(2,1)S(1)}, bf16[1,16,16,512]{3,2,1,0:T(8,128)(2,1)S(1)}, bf16[9,512,512]{2,1,0:T(8,128)(2,1)}, bf16[1,16,16,512]{3,2,1,0:T(8,128)(2,1)S(1)}, bf16[3,512,512]{2,1,0:T(8,128)(2,1)S(1)}, ...), branch_computations={%region_3.3_spmd, %region_4.4_spmd} | conditional | flops 1612972032 | bytes 42729508 | solution.py:118
  203.8 4.5 %collective-permute-done = bf16[1,16,16,512]{3,2,1,0:T(8,128)(2,1)S(1)} collective-permute-done((bf16[1,16,16,512]{3,2,1,0:T(8,128)(2,1)}, bf16[1,16,16,512]{3,2,1,0:T(8,128)(2,1)S(1)}, u32[]{:S(2)}, u32[]{:S(2)}) %collective-permute-start) | collective-permute-done | bytes 262176 | tf_op jit(solution)/shard_map/while/body/eval_jaxpr/ppermute | solution.py:12
  210.3 5.4 %conditional.6 = (bf16[1,16,16,512]{3,2,1,0:T(8,128)(2,1)S(1)}) conditional(s32[]{:T(128)} %convert_element_type.72, () %tuple.67, (bf16[1,16,16,512]{3,2,1,0:T(8,128)(2,1)S(1)}, bf16[9,512,512]{2,1,0:T(8,128)(2,1)}) %tuple.68), branch_computations={%region_1.1_spmd, %region_2.2_spmd} | conditional | flops 1209663488 | bytes 38010916 | solution.py:105
  215.7 6.1 %collective-permute-start.2 = (bf16[1,16,16,512]{3,2,1,0:T(8,128)(2,1)S(1)}, bf16[1,16,16,512]{3,2,1,0:T(8,128)(2,1)S(1)}, u32[]{:S(2)}, u32[]{:S(2)}) collective-permute-start(bf16[1,16,16,512]{3,2,1,0:T(8,128)(2,1)S(1)} %get-tuple-element.419), channel_id=1, source_target_pairs={{0,1},{1,2},{2,3},{3,4},{4,5},{5,6},{6,7},{7,8},{8,9},{9,10},{10,1... | collective-permute-start | bytes 786440 | tf_op jit(solution)/shard_map/while/body/eval_jaxpr/ppermute | solution.py:23
  223.1 3.1 collective-permute-done.3
  226.2 8.0 %conditional.7 = (bf16[1,16,16,512]{3,2,1,0:T(8,128)(2,1)}) conditional(s32[]{:T(128)} %convert_element_type.72, () %tuple.66, (bf16[1,16,16,512]{3,2,1,0:T(8,128)(2,1)S(1)}, bf16[1,16,16,512]{3,2,1,0:T(8,128)(2,1)S(1)}, bf16[9,512,512]{2,1,0:T(8,128)(2,1)}, bf16[1,16,16,512]{3,2,1,0:T(8,128)(2,1)S(1)}, bf16[3,512,512]{2,1,0:T(8,128)(2,1)S(1)}, ...), branch_computations={%region_3.3_spmd, %region_4.4_spmd} | conditional | flops 1612972032 | bytes 42729508 | solution.py:118
  236.5 4.3 %collective-permute-start.1 = (bf16[1,1,16,16,512]{4,3,2,1,0:T(8,128)(2,1)S(1)}, bf16[1,1,16,16,512]{4,3,2,1,0:T(8,128)(2,1)S(1)}, u32[]{:S(2)}, u32[]{:S(2)}) collective-permute-start(bf16[1,1,16,16,512]{4,3,2,1,0:T(8,128)(2,1)S(1)} %broadcast_select_fusion.3), channel_id=1, source_target_pairs={{0,16},{1,17},{2,18},{3,19},{4,20},{5,21},{6,22},{7,23},{8,24},{9,... | collective-permute-start | bytes 786440 | tf_op jit(solution)/shard_map/while/body/eval_jaxpr/ppermute | solution.py:12
  244.7 3.7 collective-permute-done
  250.3 5.4 %conditional.6 = (bf16[1,16,16,512]{3,2,1,0:T(8,128)(2,1)S(1)}) conditional(s32[]{:T(128)} %convert_element_type.72, () %tuple.67, (bf16[1,16,16,512]{3,2,1,0:T(8,128)(2,1)S(1)}, bf16[9,512,512]{2,1,0:T(8,128)(2,1)}) %tuple.68), branch_computations={%region_1.1_spmd, %region_2.2_spmd} | conditional | flops 1209663488 | bytes 38010916 | solution.py:105
  255.7 6.9 %collective-permute-start.2 = (bf16[1,16,16,512]{3,2,1,0:T(8,128)(2,1)S(1)}, bf16[1,16,16,512]{3,2,1,0:T(8,128)(2,1)S(1)}, u32[]{:S(2)}, u32[]{:S(2)}) collective-permute-start(bf16[1,16,16,512]{3,2,1,0:T(8,128)(2,1)S(1)} %get-tuple-element.419), channel_id=1, source_target_pairs={{0,1},{1,2},{2,3},{3,4},{4,5},{5,6},{6,7},{7,8},{8,9},{9,10},{10,1... | collective-permute-start | bytes 786440 | tf_op jit(solution)/shard_map/while/body/eval_jaxpr/ppermute | solution.py:23
  263.9 3.1 collective-permute-done.3
  267.0 8.0 %conditional.7 = (bf16[1,16,16,512]{3,2,1,0:T(8,128)(2,1)}) conditional(s32[]{:T(128)} %convert_element_type.72, () %tuple.66, (bf16[1,16,16,512]{3,2,1,0:T(8,128)(2,1)S(1)}, bf16[1,16,16,512]{3,2,1,0:T(8,128)(2,1)S(1)}, bf16[9,512,512]{2,1,0:T(8,128)(2,1)}, bf16[1,16,16,512]{3,2,1,0:T(8,128)(2,1)S(1)}, bf16[3,512,512]{2,1,0:T(8,128)(2,1)S(1)}, ...), branch_computations={%region_3.3_spmd, %region_4.4_spmd} | conditional | flops 1612972032 | bytes 42729508 | solution.py:118
  277.3 4.3 %collective-permute-start.1 = (bf16[1,1,16,16,512]{4,3,2,1,0:T(8,128)(2,1)S(1)}, bf16[1,1,16,16,512]{4,3,2,1,0:T(8,128)(2,1)S(1)}, u32[]{:S(2)}, u32[]{:S(2)}) collective-permute-start(bf16[1,1,16,16,512]{4,3,2,1,0:T(8,128)(2,1)S(1)} %broadcast_select_fusion.3), channel_id=1, source_target_pairs={{0,16},{1,17},{2,18},{3,19},{4,20},{5,21},{6,22},{7,23},{8,24},{9,... | collective-permute-start | bytes 786440 | tf_op jit(solution)/shard_map/while/body/eval_jaxpr/ppermute | solution.py:12
  285.5 2.9 collective-permute-done
  290.3 5.4 %conditional.6 = (bf16[1,16,16,512]{3,2,1,0:T(8,128)(2,1)S(1)}) conditional(s32[]{:T(128)} %convert_element_type.72, () %tuple.67, (bf16[1,16,16,512]{3,2,1,0:T(8,128)(2,1)S(1)}, bf16[9,512,512]{2,1,0:T(8,128)(2,1)}) %tuple.68), branch_computations={%region_1.1_spmd, %region_2.2_spmd} | conditional | flops 1209663488 | bytes 38010916 | solution.py:105
  295.8 8.5 %collective-permute-start.2 = (bf16[1,16,16,512]{3,2,1,0:T(8,128)(2,1)S(1)}, bf16[1,16,16,512]{3,2,1,0:T(8,128)(2,1)S(1)}, u32[]{:S(2)}, u32[]{:S(2)}) collective-permute-start(bf16[1,16,16,512]{3,2,1,0:T(8,128)(2,1)S(1)} %get-tuple-element.419), channel_id=1, source_target_pairs={{0,1},{1,2},{2,3},{3,4},{4,5},{5,6},{6,7},{7,8},{8,9},{9,10},{10,1... | collective-permute-start | bytes 786440 | tf_op jit(solution)/shard_map/while/body/eval_jaxpr/ppermute | solution.py:23
  305.7 6.1 %collective-permute-done.3 = bf16[1,16,16,512]{3,2,1,0:T(8,128)(2,1)} collective-permute-done((bf16[1,16,16,512]{3,2,1,0:T(8,128)(2,1)S(1)}, bf16[1,16,16,512]{3,2,1,0:T(8,128)(2,1)}, u32[]{:S(2)}, u32[]{:S(2)}) %collective-permute-start.3) | collective-permute-done | bytes 262176 | tf_op jit(solution)/shard_map/while/body/eval_jaxpr/ppermute | solution.py:25
  311.7 8.0 %conditional.7 = (bf16[1,16,16,512]{3,2,1,0:T(8,128)(2,1)}) conditional(s32[]{:T(128)} %convert_element_type.72, () %tuple.66, (bf16[1,16,16,512]{3,2,1,0:T(8,128)(2,1)S(1)}, bf16[1,16,16,512]{3,2,1,0:T(8,128)(2,1)S(1)}, bf16[9,512,512]{2,1,0:T(8,128)(2,1)}, bf16[1,16,16,512]{3,2,1,0:T(8,128)(2,1)S(1)}, bf16[3,512,512]{2,1,0:T(8,128)(2,1)S(1)}, ...), branch_computations={%region_3.3_spmd, %region_4.4_spmd} | conditional | flops 1612972032 | bytes 42729508 | solution.py:118
  322.0 4.3 %collective-permute-start.1 = (bf16[1,1,16,16,512]{4,3,2,1,0:T(8,128)(2,1)S(1)}, bf16[1,1,16,16,512]{4,3,2,1,0:T(8,128)(2,1)S(1)}, u32[]{:S(2)}, u32[]{:S(2)}) collective-permute-start(bf16[1,1,16,16,512]{4,3,2,1,0:T(8,128)(2,1)S(1)} %broadcast_select_fusion.3), channel_id=1, source_target_pairs={{0,16},{1,17},{2,18},{3,19},{4,20},{5,21},{6,22},{7,23},{8,24},{9,... | collective-permute-start | bytes 786440 | tf_op jit(solution)/shard_map/while/body/eval_jaxpr/ppermute | solution.py:12
  330.2 2.9 collective-permute-done
  335.1 8.5 %collective-permute-start.2 = (bf16[1,16,16,512]{3,2,1,0:T(8,128)(2,1)S(1)}, bf16[1,16,16,512]{3,2,1,0:T(8,128)(2,1)S(1)}, u32[]{:S(2)}, u32[]{:S(2)}) collective-permute-start(bf16[1,16,16,512]{3,2,1,0:T(8,128)(2,1)S(1)} %get-tuple-element.419), channel_id=1, source_target_pairs={{0,1},{1,2},{2,3},{3,4},{4,5},{5,6},{6,7},{7,8},{8,9},{9,10},{10,1... | collective-permute-start | bytes 786440 | tf_op jit(solution)/shard_map/while/body/eval_jaxpr/ppermute | solution.py:23
  345.0 6.1 %collective-permute-done.3 = bf16[1,16,16,512]{3,2,1,0:T(8,128)(2,1)} collective-permute-done((bf16[1,16,16,512]{3,2,1,0:T(8,128)(2,1)S(1)}, bf16[1,16,16,512]{3,2,1,0:T(8,128)(2,1)}, u32[]{:S(2)}, u32[]{:S(2)}) %collective-permute-start.3) | collective-permute-done | bytes 262176 | tf_op jit(solution)/shard_map/while/body/eval_jaxpr/ppermute | solution.py:25
  354.2 66.0 %all-reduce.4.cloned.1.call-done = bf16[4,1,16,16,512]{4,3,2,1,0:T(8,128)(2,1)} async-done(((bf16[4,1,16,16,512]{4,3,2,1,0:T(8,128)(2,1)}), bf16[4,1,16,16,512]{4,3,2,1,0:T(8,128)(2,1)}) %all-reduce.4.cloned.1.call-update) | async-done | bytes 1048592 | tf_op jit(solution)/shard_map/psum | solution.py:34
  (186 shorter events, 104.2 us)
Async XLA Ops:
  6.5 45.4 %all-gather.8.cloned.1.call-start = ((), (), s32[]{:S(2)}) async-start(), calls=%async_computation.2 | async-start | bytes 1671168 | tf_op jit(solution)/shard_map/all_gather | solution.py:71
  7.3 98.5 %all-gather.4.cloned.1.call-start = ((), (), s32[]{:S(2)}) async-start(), calls=%async_computation | async-start | bytes 5013504 | tf_op jit(solution)/shard_map/all_gather | solution.py:69
  8.0 151.5 %all-gather.6.cloned.1.call-start = ((), (), s32[]{:S(2)}) async-start(), calls=%async_computation.1 | async-start | bytes 5013504 | tf_op jit(solution)/shard_map/all_gather | solution.py:70
  8.7 411.5 %all-reduce.4.cloned.1.call-start = ((), (), s32[]{:S(2)}) async-start(), calls=%async_computation.3 | async-start | bytes 2097152 | tf_op jit(solution)/shard_map/psum | solution.py:34
  160.3 10.1 %collective-permute-start.1 = (bf16[1,1,16,16,512]{4,3,2,1,0:T(8,128)(2,1)S(1)}, bf16[1,1,16,16,512]{4,3,2,1,0:T(8,128)(2,1)S(1)}, u32[]{:S(2)}, u32[]{:S(2)}) collective-permute-start(bf16[1,1,16,16,512]{4,3,2,1,0:T(8,128)(2,1)S(1)} %broadcast_select_fusion.3), channel_id=1, source_target_pairs={{0,16},{1,17},{2,18},{3,19},{4,20},{5,21},{6,22},{7,23},{8,24},{9,... | collective-permute-start | bytes 786440 | tf_op jit(solution)/shard_map/while/body/eval_jaxpr/ppermute | solution.py:12
  163.7 11.7 %collective-permute-start = (bf16[1,16,16,512]{3,2,1,0:T(8,128)(2,1)}, bf16[1,16,16,512]{3,2,1,0:T(8,128)(2,1)S(1)}, u32[]{:S(2)}, u32[]{:S(2)}) collective-permute-start(bf16[1,16,16,512]{3,2,1,0:T(8,128)(2,1)} %get-tuple-element.384), channel_id=1, source_target_pairs={{0,16},{1,17},{2,18},{3,19},{4,20},{5,21},{6,22},{7,23},{8,24},{9,... | collective-permute-start | bytes 786440 | tf_op jit(solution)/shard_map/while/body/eval_jaxpr/ppermute | solution.py:12
  175.3 13.0 %copy-start.2 = (bf16[3,512,512]{2,1,0:T(8,128)(2,1)S(1)}, bf16[3,512,512]{2,1,0:T(8,128)(2,1)}, u32[]{:S(2)}) copy-start(bf16[3,512,512]{2,1,0:T(8,128)(2,1)} %get-tuple-element.414) | copy-start | bytes 4718596 | tf_op jit(solution)/shard_map/while
  182.7 2.6 collective-permute-start.2
  184.1 4.3 %collective-permute-start.3 = (bf16[1,16,16,512]{3,2,1,0:T(8,128)(2,1)S(1)}, bf16[1,16,16,512]{3,2,1,0:T(8,128)(2,1)}, u32[]{:S(2)}, u32[]{:S(2)}) collective-permute-start(bf16[1,16,16,512]{3,2,1,0:T(8,128)(2,1)S(1)} %get-tuple-element.419), channel_id=1, source_target_pairs={{1,0},{2,1},{3,2},{4,3},{5,4},{6,5},{7,6},{8,7},{9,8},{10,9},{11,1... | collective-permute-start | bytes 786440 | tf_op jit(solution)/shard_map/while/body/eval_jaxpr/ppermute | solution.py:25
  188.4 3.1 copy-start.1
  198.7 5.2 %collective-permute-start.1 = (bf16[1,1,16,16,512]{4,3,2,1,0:T(8,128)(2,1)S(1)}, bf16[1,1,16,16,512]{4,3,2,1,0:T(8,128)(2,1)S(1)}, u32[]{:S(2)}, u32[]{:S(2)}) collective-permute-start(bf16[1,1,16,16,512]{4,3,2,1,0:T(8,128)(2,1)S(1)} %broadcast_select_fusion.3), channel_id=1, source_target_pairs={{0,16},{1,17},{2,18},{3,19},{4,20},{5,21},{6,22},{7,23},{8,24},{9,... | collective-permute-start | bytes 786440 | tf_op jit(solution)/shard_map/while/body/eval_jaxpr/ppermute | solution.py:12
  200.0 8.3 %collective-permute-start = (bf16[1,16,16,512]{3,2,1,0:T(8,128)(2,1)}, bf16[1,16,16,512]{3,2,1,0:T(8,128)(2,1)S(1)}, u32[]{:S(2)}, u32[]{:S(2)}) collective-permute-start(bf16[1,16,16,512]{3,2,1,0:T(8,128)(2,1)} %get-tuple-element.384), channel_id=1, source_target_pairs={{0,16},{1,17},{2,18},{3,19},{4,20},{5,21},{6,22},{7,23},{8,24},{9,... | collective-permute-start | bytes 786440 | tf_op jit(solution)/shard_map/while/body/eval_jaxpr/ppermute | solution.py:12
  208.3 17.9 %copy-start.2 = (bf16[3,512,512]{2,1,0:T(8,128)(2,1)S(1)}, bf16[3,512,512]{2,1,0:T(8,128)(2,1)}, u32[]{:S(2)}) copy-start(bf16[3,512,512]{2,1,0:T(8,128)(2,1)} %get-tuple-element.414) | copy-start | bytes 4718596 | tf_op jit(solution)/shard_map/while
  215.7 7.4 %collective-permute-start.2 = (bf16[1,16,16,512]{3,2,1,0:T(8,128)(2,1)S(1)}, bf16[1,16,16,512]{3,2,1,0:T(8,128)(2,1)S(1)}, u32[]{:S(2)}, u32[]{:S(2)}) collective-permute-start(bf16[1,16,16,512]{3,2,1,0:T(8,128)(2,1)S(1)} %get-tuple-element.419), channel_id=1, source_target_pairs={{0,1},{1,2},{2,3},{3,4},{4,5},{5,6},{6,7},{7,8},{8,9},{9,10},{10,1... | collective-permute-start | bytes 786440 | tf_op jit(solution)/shard_map/while/body/eval_jaxpr/ppermute | solution.py:23
  221.8 4.4 %collective-permute-start.3 = (bf16[1,16,16,512]{3,2,1,0:T(8,128)(2,1)S(1)}, bf16[1,16,16,512]{3,2,1,0:T(8,128)(2,1)}, u32[]{:S(2)}, u32[]{:S(2)}) collective-permute-start(bf16[1,16,16,512]{3,2,1,0:T(8,128)(2,1)S(1)} %get-tuple-element.419), channel_id=1, source_target_pairs={{1,0},{2,1},{3,2},{4,3},{5,4},{6,5},{7,6},{8,7},{9,8},{10,9},{11,1... | collective-permute-start | bytes 786440 | tf_op jit(solution)/shard_map/while/body/eval_jaxpr/ppermute | solution.py:25
  226.2 3.1 copy-start.1
  236.5 8.2 %collective-permute-start.1 = (bf16[1,1,16,16,512]{4,3,2,1,0:T(8,128)(2,1)S(1)}, bf16[1,1,16,16,512]{4,3,2,1,0:T(8,128)(2,1)S(1)}, u32[]{:S(2)}, u32[]{:S(2)}) collective-permute-start(bf16[1,1,16,16,512]{4,3,2,1,0:T(8,128)(2,1)S(1)} %broadcast_select_fusion.3), channel_id=1, source_target_pairs={{0,16},{1,17},{2,18},{3,19},{4,20},{5,21},{6,22},{7,23},{8,24},{9,... | collective-permute-start | bytes 786440 | tf_op jit(solution)/shard_map/while/body/eval_jaxpr/ppermute | solution.py:12
  240.8 7.5 %collective-permute-start = (bf16[1,16,16,512]{3,2,1,0:T(8,128)(2,1)}, bf16[1,16,16,512]{3,2,1,0:T(8,128)(2,1)S(1)}, u32[]{:S(2)}, u32[]{:S(2)}) collective-permute-start(bf16[1,16,16,512]{3,2,1,0:T(8,128)(2,1)} %get-tuple-element.384), channel_id=1, source_target_pairs={{0,16},{1,17},{2,18},{3,19},{4,20},{5,21},{6,22},{7,23},{8,24},{9,... | collective-permute-start | bytes 786440 | tf_op jit(solution)/shard_map/while/body/eval_jaxpr/ppermute | solution.py:12
  248.3 18.7 %copy-start.2 = (bf16[3,512,512]{2,1,0:T(8,128)(2,1)S(1)}, bf16[3,512,512]{2,1,0:T(8,128)(2,1)}, u32[]{:S(2)}) copy-start(bf16[3,512,512]{2,1,0:T(8,128)(2,1)} %get-tuple-element.414) | copy-start | bytes 4718596 | tf_op jit(solution)/shard_map/while
  255.7 8.2 %collective-permute-start.2 = (bf16[1,16,16,512]{3,2,1,0:T(8,128)(2,1)S(1)}, bf16[1,16,16,512]{3,2,1,0:T(8,128)(2,1)S(1)}, u32[]{:S(2)}, u32[]{:S(2)}) collective-permute-start(bf16[1,16,16,512]{3,2,1,0:T(8,128)(2,1)S(1)} %get-tuple-element.419), channel_id=1, source_target_pairs={{0,1},{1,2},{2,3},{3,4},{4,5},{5,6},{6,7},{7,8},{8,9},{9,10},{10,1... | collective-permute-start | bytes 786440 | tf_op jit(solution)/shard_map/while/body/eval_jaxpr/ppermute | solution.py:23
  262.6 4.4 %collective-permute-start.3 = (bf16[1,16,16,512]{3,2,1,0:T(8,128)(2,1)S(1)}, bf16[1,16,16,512]{3,2,1,0:T(8,128)(2,1)}, u32[]{:S(2)}, u32[]{:S(2)}) collective-permute-start(bf16[1,16,16,512]{3,2,1,0:T(8,128)(2,1)S(1)} %get-tuple-element.419), channel_id=1, source_target_pairs={{1,0},{2,1},{3,2},{4,3},{5,4},{6,5},{7,6},{8,7},{9,8},{10,9},{11,1... | collective-permute-start | bytes 786440 | tf_op jit(solution)/shard_map/while/body/eval_jaxpr/ppermute | solution.py:25
  267.0 3.1 copy-start.1
  277.3 8.2 %collective-permute-start.1 = (bf16[1,1,16,16,512]{4,3,2,1,0:T(8,128)(2,1)S(1)}, bf16[1,1,16,16,512]{4,3,2,1,0:T(8,128)(2,1)S(1)}, u32[]{:S(2)}, u32[]{:S(2)}) collective-permute-start(bf16[1,1,16,16,512]{4,3,2,1,0:T(8,128)(2,1)S(1)} %broadcast_select_fusion.3), channel_id=1, source_target_pairs={{0,16},{1,17},{2,18},{3,19},{4,20},{5,21},{6,22},{7,23},{8,24},{9,... | collective-permute-start | bytes 786440 | tf_op jit(solution)/shard_map/while/body/eval_jaxpr/ppermute | solution.py:12
  281.6 6.8 %collective-permute-start = (bf16[1,16,16,512]{3,2,1,0:T(8,128)(2,1)}, bf16[1,16,16,512]{3,2,1,0:T(8,128)(2,1)S(1)}, u32[]{:S(2)}, u32[]{:S(2)}) collective-permute-start(bf16[1,16,16,512]{3,2,1,0:T(8,128)(2,1)} %get-tuple-element.384), channel_id=1, source_target_pairs={{0,16},{1,17},{2,18},{3,19},{4,20},{5,21},{6,22},{7,23},{8,24},{9,... | collective-permute-start | bytes 786440 | tf_op jit(solution)/shard_map/while/body/eval_jaxpr/ppermute | solution.py:12
  288.4 23.3 %copy-start.2 = (bf16[3,512,512]{2,1,0:T(8,128)(2,1)S(1)}, bf16[3,512,512]{2,1,0:T(8,128)(2,1)}, u32[]{:S(2)}) copy-start(bf16[3,512,512]{2,1,0:T(8,128)(2,1)} %get-tuple-element.414) | copy-start | bytes 4718596 | tf_op jit(solution)/shard_map/while
  295.8 9.9 %collective-permute-start.2 = (bf16[1,16,16,512]{3,2,1,0:T(8,128)(2,1)S(1)}, bf16[1,16,16,512]{3,2,1,0:T(8,128)(2,1)S(1)}, u32[]{:S(2)}, u32[]{:S(2)}) collective-permute-start(bf16[1,16,16,512]{3,2,1,0:T(8,128)(2,1)S(1)} %get-tuple-element.419), channel_id=1, source_target_pairs={{0,1},{1,2},{2,3},{3,4},{4,5},{5,6},{6,7},{7,8},{8,9},{9,10},{10,1... | collective-permute-start | bytes 786440 | tf_op jit(solution)/shard_map/while/body/eval_jaxpr/ppermute | solution.py:23
  304.3 7.4 %collective-permute-start.3 = (bf16[1,16,16,512]{3,2,1,0:T(8,128)(2,1)S(1)}, bf16[1,16,16,512]{3,2,1,0:T(8,128)(2,1)}, u32[]{:S(2)}, u32[]{:S(2)}) collective-permute-start(bf16[1,16,16,512]{3,2,1,0:T(8,128)(2,1)S(1)} %get-tuple-element.419), channel_id=1, source_target_pairs={{1,0},{2,1},{3,2},{4,3},{5,4},{6,5},{7,6},{8,7},{9,8},{10,9},{11,1... | collective-permute-start | bytes 786440 | tf_op jit(solution)/shard_map/while/body/eval_jaxpr/ppermute | solution.py:25
  322.0 8.2 %collective-permute-start.1 = (bf16[1,1,16,16,512]{4,3,2,1,0:T(8,128)(2,1)S(1)}, bf16[1,1,16,16,512]{4,3,2,1,0:T(8,128)(2,1)S(1)}, u32[]{:S(2)}, u32[]{:S(2)}) collective-permute-start(bf16[1,1,16,16,512]{4,3,2,1,0:T(8,128)(2,1)S(1)} %broadcast_select_fusion.3), channel_id=1, source_target_pairs={{0,16},{1,17},{2,18},{3,19},{4,20},{5,21},{6,22},{7,23},{8,24},{9,... | collective-permute-start | bytes 786440 | tf_op jit(solution)/shard_map/while/body/eval_jaxpr/ppermute | solution.py:12
  326.3 6.8 %collective-permute-start = (bf16[1,16,16,512]{3,2,1,0:T(8,128)(2,1)}, bf16[1,16,16,512]{3,2,1,0:T(8,128)(2,1)S(1)}, u32[]{:S(2)}, u32[]{:S(2)}) collective-permute-start(bf16[1,16,16,512]{3,2,1,0:T(8,128)(2,1)} %get-tuple-element.384), channel_id=1, source_target_pairs={{0,16},{1,17},{2,18},{3,19},{4,20},{5,21},{6,22},{7,23},{8,24},{9,... | collective-permute-start | bytes 786440 | tf_op jit(solution)/shard_map/while/body/eval_jaxpr/ppermute | solution.py:12
  333.1 17.9 %copy-start.2 = (bf16[3,512,512]{2,1,0:T(8,128)(2,1)S(1)}, bf16[3,512,512]{2,1,0:T(8,128)(2,1)}, u32[]{:S(2)}) copy-start(bf16[3,512,512]{2,1,0:T(8,128)(2,1)} %get-tuple-element.414) | copy-start | bytes 4718596 | tf_op jit(solution)/shard_map/while
  335.1 9.9 %collective-permute-start.2 = (bf16[1,16,16,512]{3,2,1,0:T(8,128)(2,1)S(1)}, bf16[1,16,16,512]{3,2,1,0:T(8,128)(2,1)S(1)}, u32[]{:S(2)}, u32[]{:S(2)}) collective-permute-start(bf16[1,16,16,512]{3,2,1,0:T(8,128)(2,1)S(1)} %get-tuple-element.419), channel_id=1, source_target_pairs={{0,1},{1,2},{2,3},{3,4},{4,5},{5,6},{6,7},{7,8},{8,9},{9,10},{10,1... | collective-permute-start | bytes 786440 | tf_op jit(solution)/shard_map/while/body/eval_jaxpr/ppermute | solution.py:23
  343.6 7.4 %collective-permute-start.3 = (bf16[1,16,16,512]{3,2,1,0:T(8,128)(2,1)S(1)}, bf16[1,16,16,512]{3,2,1,0:T(8,128)(2,1)}, u32[]{:S(2)}, u32[]{:S(2)}) collective-permute-start(bf16[1,16,16,512]{3,2,1,0:T(8,128)(2,1)S(1)} %get-tuple-element.419), channel_id=1, source_target_pairs={{1,0},{2,1},{3,2},{4,3},{5,4},{6,5},{7,6},{8,7},{9,8},{10,9},{11,1... | collective-permute-start | bytes 786440 | tf_op jit(solution)/shard_map/while/body/eval_jaxpr/ppermute | solution.py:25
  (5 other events, 15.7 us)
Sparse Core Ops, SparseCore 0:
  9.5 42.3 all-gather.7
  54.1 51.6 all-gather.3
  108.0 51.4 all-gather.5
  354.3 65.8 all-reduce.3
where the time goes:
time: 430 us; the launch traced here: 429 us
  waiting for transfers between devices  268 us (62%)
  starting transfers between devices  62.1 us (14%)
  matrix products  50 us (12%)
  other arithmetic  22 us (5%)
  between operations  13.2 us (3%)
  local copies, waits for them, and re-layouts  8.96 us (2%)
  loops' own time  4.66 us (1%)
    psum x1, waiting for transfers between devices, broadcast(): return lax.psum(jnp.where(mine, shard, jnp.zeros_like(shard)), axis)  66 us
    all_gather x1, waiting for transfers between devices, on_device(): lax.all_gather(conv_first, 'frame', axis=2, tiled=True)  53.9 us
    all_gather x1, waiting for transfers between devices, on_device(): lax.all_gather(conv_second, 'frame', axis=2, tiled=True)  53.7 us
    all_gather x1, waiting for transfers between devices, on_device(): lax.all_gather(temporal, 'frame', axis=2, tiled=True)  43.1 us
    dot_general x72, matrix products, spatial(): jnp.dot(window, kernel[3 * row_shift + col_shift], preferred_element_type...  39.4 us
    ppermute x5, starting transfers between devices, extended_2(): lax.ppermute(tail, axis, [(i, (i + 1) % count) for i in range(ends)])  31.4 us
    ppermute x10, waiting for transfers between devices, passed_along(): return lax.ppermute(shard, axis, pairs)  27.6 us
    ppermute x10, starting transfers between devices, passed_along(): return lax.ppermute(shard, axis, pairs)  24.1 us
  transfers between devices with their start and end apart: 24, of which 19 were waited for; matrix products, arithmetic and copies ran while one was open for 1% of the time, Pallas kernels for 0%

commit v1 on v0

--- a/solution.py
+++ b/solution.py
@@ -66,7 +66,7 @@
     sections = lax.axis_size("segment")
     segment_id = lax.axis_index("segment")
     first_full, second_full, time_full = (
-        lax.all_gather(conv_first, "frame", axis=2, tiled=True),
+        jnp.concatenate(lax.all_gather(conv_first, "frame"), axis=2),
         lax.all_gather(conv_second, "frame", axis=2, tiled=True),
         lax.all_gather(temporal, "frame", axis=2, tiled=True),
     )

time: 430 us -> 430 us (level)
  local copies, waits for them, and re-layouts: 8.96 us -> 13.8 us
    all_gather x1, waiting for transfers between devices: 43.1 us -> 35.2 us  [on_device(): lax.all_gather(temporal, 'frame', axis=2, tiled=True)]
    all_gather x0 -> x1, local copies, waits for them, and re-layouts: none -> 5.23 us  [on_device(): lax.all_gather(conv_first, 'frame')]
  transfers between devices with their start and end apart: 24 -> 24, of which waited for: 19 -> 19; matrix products, arithmetic and copies ran while one was open for 1% -> 2% of each run, Pallas kernels for 0% -> 0%
where the time goes in v1:
time: 430 us; the launch traced here: 429 us
  waiting for transfers between devices  264 us (61%)
  starting transfers between devices  62.1 us (14%)
  matrix products  50 us (12%)
  other arithmetic  22 us (5%)
  local copies, waits for them, and re-layouts  13.8 us (3%)
  between operations  13.2 us (3%)
    psum x1, waiting for transfers between devices, broadcast(): return lax.psum(jnp.where(mine, shard, jnp.zeros_like(shard)), axis)  66 us
    all_gather x1, waiting for transfers between devices, on_device(): lax.all_gather(conv_first, 'frame')  56.7 us
    all_gather x1, waiting for transfers between devices, on_device(): lax.all_gather(conv_second, 'frame', axis=2, tiled=True)  53.9 us
    dot_general x72, matrix products, spatial(): jnp.dot(window, kernel[3 * row_shift + col_shift], preferred_element_type...  39.3 us
    all_gather x1, waiting for transfers between devices, on_device(): lax.all_gather(temporal, 'frame', axis=2, tiled=True)  35.2 us
    ppermute x5, starting transfers between devices, extended_2(): lax.ppermute(tail, axis, [(i, (i + 1) % count) for i in range(ends)])  31.4 us
    ppermute x10, waiting for transfers between devices, passed_along(): return lax.ppermute(shard, axis, pairs)  28.7 us
    ppermute x10, starting transfers between devices, passed_along(): return lax.ppermute(shard, axis, pairs)  24.1 us
  transfers between devices with their start and end apart: 24, of which 19 were waited for; matrix products, arithmetic and copies ran while one was open for 2% of the time, Pallas kernels for 0%

profile of v1, /device:TPU:0, one launch (start us, length us, event | category | flops | bytes accessed | tf_op | source)
XLA Modules:
  0.0 428.8 jit_solution(4717403278546231856)
XLA Ops:
  8.8 56.7 %all-gather.9.cloned.1.call-done = bf16[16,9,32,512]{3,2,1,0:T(8,128)(2,1)} async-done(((bf16[1,9,32,512]{3,2,1,0:T(8,128)(2,1)}), bf16[16,9,32,512]{3,2,1,0:T(8,128)(2,1)}) %all-gather.9.cloned.1.call-update) | async-done | bytes 4718608 | tf_op jit(solution)/shard_map/all_gather | solution.py:69
  65.5 5.2 %copy.6 = bf16[16,9,32,512]{3,2,0,1:T(8,128)(2,1)} copy(bf16[16,9,32,512]{3,2,1,0:T(8,128)(2,1)} %all-gather.9.cloned.1.call-done) | data formatting | bytes 9437184 | tf_op jit(solution)/shard_map/all_gather | solution.py:69
  70.7 35.2 %all-gather.7.cloned.1.call-done = bf16[1,3,512,512]{3,2,1,0:T(8,128)(2,1)} async-done(((bf16[1,3,32,512]{3,2,1,0:T(8,128)(2,1)}), bf16[1,3,512,512]{3,2,1,0:T(8,128)(2,1)}) %all-gather.7.cloned.1.call-update) | async-done | bytes 1572880 | tf_op jit(solution)/shard_map/all_gather | solution.py:71
  105.9 53.9 %all-gather.5.cloned.1.call-done = bf16[1,9,512,512]{3,2,1,0:T(8,128)(2,1)} async-done(((bf16[1,9,32,512]{3,2,1,0:T(8,128)(2,1)}), bf16[1,9,512,512]{3,2,1,0:T(8,128)(2,1)}) %all-gather.5.cloned.1.call-update) | async-done | bytes 4718608 | tf_op jit(solution)/shard_map/all_gather | solution.py:70
  160.5 192.8 %while.17 = (s32[]{:T(128)}, bf16[1,16,16,512]{3,2,1,0:T(8,128)(2,1)}, bf16[1,1,16,16,512]{4,3,2,1,0:T(8,128)(2,1)}, bf16[4,1,16,16,512]{4,3,2,1,0:T(8,128)(2,1)...) while((s32[]{:T(128)}, ...), condition=%wide.region_5.6_spmd.clone, body=%wide.region_0.5_spmd.clone.sunk | while | flops 2824994816 | bytes 95421016 | solution.py:123
  160.5 3.4 collective-permute-start.1
  166.4 4.2 collective-permute-done.1
  170.6 5.0 %collective-permute-done = bf16[1,16,16,512]{3,2,1,0:T(8,128)(2,1)S(1)} collective-permute-done((bf16[1,16,16,512]{3,2,1,0:T(8,128)(2,1)}, bf16[1,16,16,512]{3,2,1,0:T(8,128)(2,1)S(1)}, u32[]{:S(2)}, u32[]{:S(2)}) %collective-permute-start) | collective-permute-done | bytes 262176 | tf_op jit(solution)/shard_map/while/body/eval_jaxpr/ppermute | solution.py:12
  177.6 5.4 %conditional.6 = (bf16[1,16,16,512]{3,2,1,0:T(8,128)(2,1)S(1)}) conditional(s32[]{:T(128)} %convert_element_type.72, () %tuple.67, (bf16[1,16,16,512]{3,2,1,0:T(8,128)(2,1)S(1)}, bf16[9,512,512]{2,1,0:T(8,128)(2,1)}) %tuple.68), branch_computations={%region_1.1_spmd, %region_2.2_spmd} | conditional | flops 1209663488 | bytes 38010916 | solution.py:105
  185.6 3.0 collective-permute-done.3
  188.7 8.0 %conditional.7 = (bf16[1,16,16,512]{3,2,1,0:T(8,128)(2,1)}) conditional(s32[]{:T(128)} %convert_element_type.72, () %tuple.66, (bf16[1,16,16,512]{3,2,1,0:T(8,128)(2,1)S(1)}, bf16[1,16,16,512]{3,2,1,0:T(8,128)(2,1)S(1)}, bf16[9,512,512]{2,1,0:T(8,128)(2,1)}, bf16[1,16,16,512]{3,2,1,0:T(8,128)(2,1)S(1)}, bf16[3,512,512]{2,1,0:T(8,128)(2,1)S(1)}, ...), branch_computations={%region_3.3_spmd, %region_4.4_spmd} | conditional | flops 1612972032 | bytes 42729508 | solution.py:118
  204.1 4.5 %collective-permute-done = bf16[1,16,16,512]{3,2,1,0:T(8,128)(2,1)S(1)} collective-permute-done((bf16[1,16,16,512]{3,2,1,0:T(8,128)(2,1)}, bf16[1,16,16,512]{3,2,1,0:T(8,128)(2,1)S(1)}, u32[]{:S(2)}, u32[]{:S(2)}) %collective-permute-start) | collective-permute-done | bytes 262176 | tf_op jit(solution)/shard_map/while/body/eval_jaxpr/ppermute | solution.py:12
  210.5 5.4 %conditional.6 = (bf16[1,16,16,512]{3,2,1,0:T(8,128)(2,1)S(1)}) conditional(s32[]{:T(128)} %convert_element_type.72, () %tuple.67, (bf16[1,16,16,512]{3,2,1,0:T(8,128)(2,1)S(1)}, bf16[9,512,512]{2,1,0:T(8,128)(2,1)}) %tuple.68), branch_computations={%region_1.1_spmd, %region_2.2_spmd} | conditional | flops 1209663488 | bytes 38010916 | solution.py:105
  216.0 6.1 %collective-permute-start.2 = (bf16[1,16,16,512]{3,2,1,0:T(8,128)(2,1)S(1)}, bf16[1,16,16,512]{3,2,1,0:T(8,128)(2,1)S(1)}, u32[]{:S(2)}, u32[]{:S(2)}) collective-permute-start(bf16[1,16,16,512]{3,2,1,0:T(8,128)(2,1)S(1)} %get-tuple-element.419), channel_id=1, source_target_pairs={{0,1},{1,2},{2,3},{3,4},{4,5},{5,6},{6,7},{7,8},{8,9},{9,10},{10,1... | collective-permute-start | bytes 786440 | tf_op jit(solution)/shard_map/while/body/eval_jaxpr/ppermute | solution.py:23
  223.4 3.1 collective-permute-done.3
  226.5 8.0 %conditional.7 = (bf16[1,16,16,512]{3,2,1,0:T(8,128)(2,1)}) conditional(s32[]{:T(128)} %convert_element_type.72, () %tuple.66, (bf16[1,16,16,512]{3,2,1,0:T(8,128)(2,1)S(1)}, bf16[1,16,16,512]{3,2,1,0:T(8,128)(2,1)S(1)}, bf16[9,512,512]{2,1,0:T(8,128)(2,1)}, bf16[1,16,16,512]{3,2,1,0:T(8,128)(2,1)S(1)}, bf16[3,512,512]{2,1,0:T(8,128)(2,1)S(1)}, ...), branch_computations={%region_3.3_spmd, %region_4.4_spmd} | conditional | flops 1612972032 | bytes 42729508 | solution.py:118
  236.7 4.3 %collective-permute-start.1 = (bf16[1,1,16,16,512]{4,3,2,1,0:T(8,128)(2,1)S(1)}, bf16[1,1,16,16,512]{4,3,2,1,0:T(8,128)(2,1)S(1)}, u32[]{:S(2)}, u32[]{:S(2)}) collective-permute-start(bf16[1,1,16,16,512]{4,3,2,1,0:T(8,128)(2,1)S(1)} %broadcast_select_fusion.3), channel_id=1, source_target_pairs={{0,16},{1,17},{2,18},{3,19},{4,20},{5,21},{6,22},{7,23},{8,24},{9,... | collective-permute-start | bytes 786440 | tf_op jit(solution)/shard_map/while/body/eval_jaxpr/ppermute | solution.py:12
  244.9 3.7 collective-permute-done
  250.5 5.4 %conditional.6 = (bf16[1,16,16,512]{3,2,1,0:T(8,128)(2,1)S(1)}) conditional(s32[]{:T(128)} %convert_element_type.72, () %tuple.67, (bf16[1,16,16,512]{3,2,1,0:T(8,128)(2,1)S(1)}, bf16[9,512,512]{2,1,0:T(8,128)(2,1)}) %tuple.68), branch_computations={%region_1.1_spmd, %region_2.2_spmd} | conditional | flops 1209663488 | bytes 38010916 | solution.py:105
  256.0 6.9 %collective-permute-start.2 = (bf16[1,16,16,512]{3,2,1,0:T(8,128)(2,1)S(1)}, bf16[1,16,16,512]{3,2,1,0:T(8,128)(2,1)S(1)}, u32[]{:S(2)}, u32[]{:S(2)}) collective-permute-start(bf16[1,16,16,512]{3,2,1,0:T(8,128)(2,1)S(1)} %get-tuple-element.419), channel_id=1, source_target_pairs={{0,1},{1,2},{2,3},{3,4},{4,5},{5,6},{6,7},{7,8},{8,9},{9,10},{10,1... | collective-permute-start | bytes 786440 | tf_op jit(solution)/shard_map/while/body/eval_jaxpr/ppermute | solution.py:23
  264.2 3.1 collective-permute-done.3
  267.3 8.0 %conditional.7 = (bf16[1,16,16,512]{3,2,1,0:T(8,128)(2,1)}) conditional(s32[]{:T(128)} %convert_element_type.72, () %tuple.66, (bf16[1,16,16,512]{3,2,1,0:T(8,128)(2,1)S(1)}, bf16[1,16,16,512]{3,2,1,0:T(8,128)(2,1)S(1)}, bf16[9,512,512]{2,1,0:T(8,128)(2,1)}, bf16[1,16,16,512]{3,2,1,0:T(8,128)(2,1)S(1)}, bf16[3,512,512]{2,1,0:T(8,128)(2,1)S(1)}, ...), branch_computations={%region_3.3_spmd, %region_4.4_spmd} | conditional | flops 1612972032 | bytes 42729508 | solution.py:118
  277.5 4.3 %collective-permute-start.1 = (bf16[1,1,16,16,512]{4,3,2,1,0:T(8,128)(2,1)S(1)}, bf16[1,1,16,16,512]{4,3,2,1,0:T(8,128)(2,1)S(1)}, u32[]{:S(2)}, u32[]{:S(2)}) collective-permute-start(bf16[1,1,16,16,512]{4,3,2,1,0:T(8,128)(2,1)S(1)} %broadcast_select_fusion.3), channel_id=1, source_target_pairs={{0,16},{1,17},{2,18},{3,19},{4,20},{5,21},{6,22},{7,23},{8,24},{9,... | collective-permute-start | bytes 786440 | tf_op jit(solution)/shard_map/while/body/eval_jaxpr/ppermute | solution.py:12
  285.7 2.9 collective-permute-done
  290.6 5.4 %conditional.6 = (bf16[1,16,16,512]{3,2,1,0:T(8,128)(2,1)S(1)}) conditional(s32[]{:T(128)} %convert_element_type.72, () %tuple.67, (bf16[1,16,16,512]{3,2,1,0:T(8,128)(2,1)S(1)}, bf16[9,512,512]{2,1,0:T(8,128)(2,1)}) %tuple.68), branch_computations={%region_1.1_spmd, %region_2.2_spmd} | conditional | flops 1209663488 | bytes 38010916 | solution.py:105
  296.0 8.5 %collective-permute-start.2 = (bf16[1,16,16,512]{3,2,1,0:T(8,128)(2,1)S(1)}, bf16[1,16,16,512]{3,2,1,0:T(8,128)(2,1)S(1)}, u32[]{:S(2)}, u32[]{:S(2)}) collective-permute-start(bf16[1,16,16,512]{3,2,1,0:T(8,128)(2,1)S(1)} %get-tuple-element.419), channel_id=1, source_target_pairs={{0,1},{1,2},{2,3},{3,4},{4,5},{5,6},{6,7},{7,8},{8,9},{9,10},{10,1... | collective-permute-start | bytes 786440 | tf_op jit(solution)/shard_map/while/body/eval_jaxpr/ppermute | solution.py:23
  305.9 6.1 %collective-permute-done.3 = bf16[1,16,16,512]{3,2,1,0:T(8,128)(2,1)} collective-permute-done((bf16[1,16,16,512]{3,2,1,0:T(8,128)(2,1)S(1)}, bf16[1,16,16,512]{3,2,1,0:T(8,128)(2,1)}, u32[]{:S(2)}, u32[]{:S(2)}) %collective-permute-start.3) | collective-permute-done | bytes 262176 | tf_op jit(solution)/shard_map/while/body/eval_jaxpr/ppermute | solution.py:25
  312.0 8.0 %conditional.7 = (bf16[1,16,16,512]{3,2,1,0:T(8,128)(2,1)}) conditional(s32[]{:T(128)} %convert_element_type.72, () %tuple.66, (bf16[1,16,16,512]{3,2,1,0:T(8,128)(2,1)S(1)}, bf16[1,16,16,512]{3,2,1,0:T(8,128)(2,1)S(1)}, bf16[9,512,512]{2,1,0:T(8,128)(2,1)}, bf16[1,16,16,512]{3,2,1,0:T(8,128)(2,1)S(1)}, bf16[3,512,512]{2,1,0:T(8,128)(2,1)S(1)}, ...), branch_computations={%region_3.3_spmd, %region_4.4_spmd} | conditional | flops 1612972032 | bytes 42729508 | solution.py:118
  322.2 4.3 %collective-permute-start.1 = (bf16[1,1,16,16,512]{4,3,2,1,0:T(8,128)(2,1)S(1)}, bf16[1,1,16,16,512]{4,3,2,1,0:T(8,128)(2,1)S(1)}, u32[]{:S(2)}, u32[]{:S(2)}) collective-permute-start(bf16[1,1,16,16,512]{4,3,2,1,0:T(8,128)(2,1)S(1)} %broadcast_select_fusion.3), channel_id=1, source_target_pairs={{0,16},{1,17},{2,18},{3,19},{4,20},{5,21},{6,22},{7,23},{8,24},{9,... | collective-permute-start | bytes 786440 | tf_op jit(solution)/shard_map/while/body/eval_jaxpr/ppermute | solution.py:12
  335.3 8.5 %collective-permute-start.2 = (bf16[1,16,16,512]{3,2,1,0:T(8,128)(2,1)S(1)}, bf16[1,16,16,512]{3,2,1,0:T(8,128)(2,1)S(1)}, u32[]{:S(2)}, u32[]{:S(2)}) collective-permute-start(bf16[1,16,16,512]{3,2,1,0:T(8,128)(2,1)S(1)} %get-tuple-element.419), channel_id=1, source_target_pairs={{0,1},{1,2},{2,3},{3,4},{4,5},{5,6},{6,7},{7,8},{8,9},{9,10},{10,1... | collective-permute-start | bytes 786440 | tf_op jit(solution)/shard_map/while/body/eval_jaxpr/ppermute | solution.py:23
  345.2 6.1 %collective-permute-done.3 = bf16[1,16,16,512]{3,2,1,0:T(8,128)(2,1)} collective-permute-done((bf16[1,16,16,512]{3,2,1,0:T(8,128)(2,1)S(1)}, bf16[1,16,16,512]{3,2,1,0:T(8,128)(2,1)}, u32[]{:S(2)}, u32[]{:S(2)}) %collective-permute-start.3) | collective-permute-done | bytes 262176 | tf_op jit(solution)/shard_map/while/body/eval_jaxpr/ppermute | solution.py:25
  354.4 66.0 %all-reduce.4.cloned.1.call-done = bf16[4,1,16,16,512]{4,3,2,1,0:T(8,128)(2,1)} async-done(((bf16[4,1,16,16,512]{4,3,2,1,0:T(8,128)(2,1)}), bf16[4,1,16,16,512]{4,3,2,1,0:T(8,128)(2,1)}) %all-reduce.4.cloned.1.call-update) | async-done | bytes 1048592 | tf_op jit(solution)/shard_map/psum | solution.py:34
  (187 shorter events, 107.5 us)
Async XLA Ops:
  6.5 59.0 %all-gather.9.cloned.1.call-start = ((), (), s32[]{:S(2)}) async-start(), calls=%async_computation.3 | async-start | bytes 5013504 | tf_op jit(solution)/shard_map/all_gather | solution.py:69
  7.3 98.6 %all-gather.7.cloned.1.call-start = ((), (), s32[]{:S(2)}) async-start(), calls=%async_computation.1 | async-start | bytes 1671168 | tf_op jit(solution)/shard_map/all_gather | solution.py:71
  8.0 151.8 %all-gather.5.cloned.1.call-start = ((), (), s32[]{:S(2)}) async-start(), calls=%async_computation | async-start | bytes 5013504 | tf_op jit(solution)/shard_map/all_gather | solution.py:70
  8.7 411.7 %all-reduce.4.cloned.1.call-start = ((), (), s32[]{:S(2)}) async-start(), calls=%async_computation.2 | async-start | bytes 2097152 | tf_op jit(solution)/shard_map/psum | solution.py:34
  160.5 10.1 %collective-permute-start.1 = (bf16[1,1,16,16,512]{4,3,2,1,0:T(8,128)(2,1)S(1)}, bf16[1,1,16,16,512]{4,3,2,1,0:T(8,128)(2,1)S(1)}, u32[]{:S(2)}, u32[]{:S(2)}) collective-permute-start(bf16[1,1,16,16,512]{4,3,2,1,0:T(8,128)(2,1)S(1)} %broadcast_select_fusion.3), channel_id=1, source_target_pairs={{0,16},{1,17},{2,18},{3,19},{4,20},{5,21},{6,22},{7,23},{8,24},{9,... | collective-permute-start | bytes 786440 | tf_op jit(solution)/shard_map/while/body/eval_jaxpr/ppermute | solution.py:12
  163.9 11.7 %collective-permute-start = (bf16[1,16,16,512]{3,2,1,0:T(8,128)(2,1)}, bf16[1,16,16,512]{3,2,1,0:T(8,128)(2,1)S(1)}, u32[]{:S(2)}, u32[]{:S(2)}) collective-permute-start(bf16[1,16,16,512]{3,2,1,0:T(8,128)(2,1)} %get-tuple-element.384), channel_id=1, source_target_pairs={{0,16},{1,17},{2,18},{3,19},{4,20},{5,21},{6,22},{7,23},{8,24},{9,... | collective-permute-start | bytes 786440 | tf_op jit(solution)/shard_map/while/body/eval_jaxpr/ppermute | solution.py:12
  175.6 13.0 %copy-start.2 = (bf16[3,512,512]{2,1,0:T(8,128)(2,1)S(1)}, bf16[3,512,512]{2,1,0:T(8,128)(2,1)}, u32[]{:S(2)}) copy-start(bf16[3,512,512]{2,1,0:T(8,128)(2,1)} %get-tuple-element.414) | copy-start | bytes 4718596 | tf_op jit(solution)/shard_map/while
  183.0 2.6 collective-permute-start.2
  184.3 4.3 %collective-permute-start.3 = (bf16[1,16,16,512]{3,2,1,0:T(8,128)(2,1)S(1)}, bf16[1,16,16,512]{3,2,1,0:T(8,128)(2,1)}, u32[]{:S(2)}, u32[]{:S(2)}) collective-permute-start(bf16[1,16,16,512]{3,2,1,0:T(8,128)(2,1)S(1)} %get-tuple-element.419), channel_id=1, source_target_pairs={{1,0},{2,1},{3,2},{4,3},{5,4},{6,5},{7,6},{8,7},{9,8},{10,9},{11,1... | collective-permute-start | bytes 786440 | tf_op jit(solution)/shard_map/while/body/eval_jaxpr/ppermute | solution.py:25
  188.7 3.1 copy-start.1
  198.9 5.2 %collective-permute-start.1 = (bf16[1,1,16,16,512]{4,3,2,1,0:T(8,128)(2,1)S(1)}, bf16[1,1,16,16,512]{4,3,2,1,0:T(8,128)(2,1)S(1)}, u32[]{:S(2)}, u32[]{:S(2)}) collective-permute-start(bf16[1,1,16,16,512]{4,3,2,1,0:T(8,128)(2,1)S(1)} %broadcast_select_fusion.3), channel_id=1, source_target_pairs={{0,16},{1,17},{2,18},{3,19},{4,20},{5,21},{6,22},{7,23},{8,24},{9,... | collective-permute-start | bytes 786440 | tf_op jit(solution)/shard_map/while/body/eval_jaxpr/ppermute | solution.py:12
  200.2 8.3 %collective-permute-start = (bf16[1,16,16,512]{3,2,1,0:T(8,128)(2,1)}, bf16[1,16,16,512]{3,2,1,0:T(8,128)(2,1)S(1)}, u32[]{:S(2)}, u32[]{:S(2)}) collective-permute-start(bf16[1,16,16,512]{3,2,1,0:T(8,128)(2,1)} %get-tuple-element.384), channel_id=1, source_target_pairs={{0,16},{1,17},{2,18},{3,19},{4,20},{5,21},{6,22},{7,23},{8,24},{9,... | collective-permute-start | bytes 786440 | tf_op jit(solution)/shard_map/while/body/eval_jaxpr/ppermute | solution.py:12
  208.6 17.9 %copy-start.2 = (bf16[3,512,512]{2,1,0:T(8,128)(2,1)S(1)}, bf16[3,512,512]{2,1,0:T(8,128)(2,1)}, u32[]{:S(2)}) copy-start(bf16[3,512,512]{2,1,0:T(8,128)(2,1)} %get-tuple-element.414) | copy-start | bytes 4718596 | tf_op jit(solution)/shard_map/while
  216.0 7.4 %collective-permute-start.2 = (bf16[1,16,16,512]{3,2,1,0:T(8,128)(2,1)S(1)}, bf16[1,16,16,512]{3,2,1,0:T(8,128)(2,1)S(1)}, u32[]{:S(2)}, u32[]{:S(2)}) collective-permute-start(bf16[1,16,16,512]{3,2,1,0:T(8,128)(2,1)S(1)} %get-tuple-element.419), channel_id=1, source_target_pairs={{0,1},{1,2},{2,3},{3,4},{4,5},{5,6},{6,7},{7,8},{8,9},{9,10},{10,1... | collective-permute-start | bytes 786440 | tf_op jit(solution)/shard_map/while/body/eval_jaxpr/ppermute | solution.py:23
  222.1 4.4 %collective-permute-start.3 = (bf16[1,16,16,512]{3,2,1,0:T(8,128)(2,1)S(1)}, bf16[1,16,16,512]{3,2,1,0:T(8,128)(2,1)}, u32[]{:S(2)}, u32[]{:S(2)}) collective-permute-start(bf16[1,16,16,512]{3,2,1,0:T(8,128)(2,1)S(1)} %get-tuple-element.419), channel_id=1, source_target_pairs={{1,0},{2,1},{3,2},{4,3},{5,4},{6,5},{7,6},{8,7},{9,8},{10,9},{11,1... | collective-permute-start | bytes 786440 | tf_op jit(solution)/shard_map/while/body/eval_jaxpr/ppermute | solution.py:25
  236.7 8.2 %collective-permute-start.1 = (bf16[1,1,16,16,512]{4,3,2,1,0:T(8,128)(2,1)S(1)}, bf16[1,1,16,16,512]{4,3,2,1,0:T(8,128)(2,1)S(1)}, u32[]{:S(2)}, u32[]{:S(2)}) collective-permute-start(bf16[1,1,16,16,512]{4,3,2,1,0:T(8,128)(2,1)S(1)} %broadcast_select_fusion.3), channel_id=1, source_target_pairs={{0,16},{1,17},{2,18},{3,19},{4,20},{5,21},{6,22},{7,23},{8,24},{9,... | collective-permute-start | bytes 786440 | tf_op jit(solution)/shard_map/while/body/eval_jaxpr/ppermute | solution.py:12
  241.0 7.5 %collective-permute-start = (bf16[1,16,16,512]{3,2,1,0:T(8,128)(2,1)}, bf16[1,16,16,512]{3,2,1,0:T(8,128)(2,1)S(1)}, u32[]{:S(2)}, u32[]{:S(2)}) collective-permute-start(bf16[1,16,16,512]{3,2,1,0:T(8,128)(2,1)} %get-tuple-element.384), channel_id=1, source_target_pairs={{0,16},{1,17},{2,18},{3,19},{4,20},{5,21},{6,22},{7,23},{8,24},{9,... | collective-permute-start | bytes 786440 | tf_op jit(solution)/shard_map/while/body/eval_jaxpr/ppermute | solution.py:12
  248.6 18.7 %copy-start.2 = (bf16[3,512,512]{2,1,0:T(8,128)(2,1)S(1)}, bf16[3,512,512]{2,1,0:T(8,128)(2,1)}, u32[]{:S(2)}) copy-start(bf16[3,512,512]{2,1,0:T(8,128)(2,1)} %get-tuple-element.414) | copy-start | bytes 4718596 | tf_op jit(solution)/shard_map/while
  256.0 8.2 %collective-permute-start.2 = (bf16[1,16,16,512]{3,2,1,0:T(8,128)(2,1)S(1)}, bf16[1,16,16,512]{3,2,1,0:T(8,128)(2,1)S(1)}, u32[]{:S(2)}, u32[]{:S(2)}) collective-permute-start(bf16[1,16,16,512]{3,2,1,0:T(8,128)(2,1)S(1)} %get-tuple-element.419), channel_id=1, source_target_pairs={{0,1},{1,2},{2,3},{3,4},{4,5},{5,6},{6,7},{7,8},{8,9},{9,10},{10,1... | collective-permute-start | bytes 786440 | tf_op jit(solution)/shard_map/while/body/eval_jaxpr/ppermute | solution.py:23
  262.9 4.4 %collective-permute-start.3 = (bf16[1,16,16,512]{3,2,1,0:T(8,128)(2,1)S(1)}, bf16[1,16,16,512]{3,2,1,0:T(8,128)(2,1)}, u32[]{:S(2)}, u32[]{:S(2)}) collective-permute-start(bf16[1,16,16,512]{3,2,1,0:T(8,128)(2,1)S(1)} %get-tuple-element.419), channel_id=1, source_target_pairs={{1,0},{2,1},{3,2},{4,3},{5,4},{6,5},{7,6},{8,7},{9,8},{10,9},{11,1... | collective-permute-start | bytes 786440 | tf_op jit(solution)/shard_map/while/body/eval_jaxpr/ppermute | solution.py:25
  267.3 3.1 copy-start.1
  277.5 8.2 %collective-permute-start.1 = (bf16[1,1,16,16,512]{4,3,2,1,0:T(8,128)(2,1)S(1)}, bf16[1,1,16,16,512]{4,3,2,1,0:T(8,128)(2,1)S(1)}, u32[]{:S(2)}, u32[]{:S(2)}) collective-permute-start(bf16[1,1,16,16,512]{4,3,2,1,0:T(8,128)(2,1)S(1)} %broadcast_select_fusion.3), channel_id=1, source_target_pairs={{0,16},{1,17},{2,18},{3,19},{4,20},{5,21},{6,22},{7,23},{8,24},{9,... | collective-permute-start | bytes 786440 | tf_op jit(solution)/shard_map/while/body/eval_jaxpr/ppermute | solution.py:12
  281.9 6.8 %collective-permute-start = (bf16[1,16,16,512]{3,2,1,0:T(8,128)(2,1)}, bf16[1,16,16,512]{3,2,1,0:T(8,128)(2,1)S(1)}, u32[]{:S(2)}, u32[]{:S(2)}) collective-permute-start(bf16[1,16,16,512]{3,2,1,0:T(8,128)(2,1)} %get-tuple-element.384), channel_id=1, source_target_pairs={{0,16},{1,17},{2,18},{3,19},{4,20},{5,21},{6,22},{7,23},{8,24},{9,... | collective-permute-start | bytes 786440 | tf_op jit(solution)/shard_map/while/body/eval_jaxpr/ppermute | solution.py:12
  288.6 23.3 %copy-start.2 = (bf16[3,512,512]{2,1,0:T(8,128)(2,1)S(1)}, bf16[3,512,512]{2,1,0:T(8,128)(2,1)}, u32[]{:S(2)}) copy-start(bf16[3,512,512]{2,1,0:T(8,128)(2,1)} %get-tuple-element.414) | copy-start | bytes 4718596 | tf_op jit(solution)/shard_map/while
  296.0 9.9 %collective-permute-start.2 = (bf16[1,16,16,512]{3,2,1,0:T(8,128)(2,1)S(1)}, bf16[1,16,16,512]{3,2,1,0:T(8,128)(2,1)S(1)}, u32[]{:S(2)}, u32[]{:S(2)}) collective-permute-start(bf16[1,16,16,512]{3,2,1,0:T(8,128)(2,1)S(1)} %get-tuple-element.419), channel_id=1, source_target_pairs={{0,1},{1,2},{2,3},{3,4},{4,5},{5,6},{6,7},{7,8},{8,9},{9,10},{10,1... | collective-permute-start | bytes 786440 | tf_op jit(solution)/shard_map/while/body/eval_jaxpr/ppermute | solution.py:23
  304.6 7.4 %collective-permute-start.3 = (bf16[1,16,16,512]{3,2,1,0:T(8,128)(2,1)S(1)}, bf16[1,16,16,512]{3,2,1,0:T(8,128)(2,1)}, u32[]{:S(2)}, u32[]{:S(2)}) collective-permute-start(bf16[1,16,16,512]{3,2,1,0:T(8,128)(2,1)S(1)} %get-tuple-element.419), channel_id=1, source_target_pairs={{1,0},{2,1},{3,2},{4,3},{5,4},{6,5},{7,6},{8,7},{9,8},{10,9},{11,1... | collective-permute-start | bytes 786440 | tf_op jit(solution)/shard_map/while/body/eval_jaxpr/ppermute | solution.py:25
  312.0 3.1 copy-start.1
  322.2 8.2 %collective-permute-start.1 = (bf16[1,1,16,16,512]{4,3,2,1,0:T(8,128)(2,1)S(1)}, bf16[1,1,16,16,512]{4,3,2,1,0:T(8,128)(2,1)S(1)}, u32[]{:S(2)}, u32[]{:S(2)}) collective-permute-start(bf16[1,1,16,16,512]{4,3,2,1,0:T(8,128)(2,1)S(1)} %broadcast_select_fusion.3), channel_id=1, source_target_pairs={{0,16},{1,17},{2,18},{3,19},{4,20},{5,21},{6,22},{7,23},{8,24},{9,... | collective-permute-start | bytes 786440 | tf_op jit(solution)/shard_map/while/body/eval_jaxpr/ppermute | solution.py:12
  326.5 6.8 %collective-permute-start = (bf16[1,16,16,512]{3,2,1,0:T(8,128)(2,1)}, bf16[1,16,16,512]{3,2,1,0:T(8,128)(2,1)S(1)}, u32[]{:S(2)}, u32[]{:S(2)}) collective-permute-start(bf16[1,16,16,512]{3,2,1,0:T(8,128)(2,1)} %get-tuple-element.384), channel_id=1, source_target_pairs={{0,16},{1,17},{2,18},{3,19},{4,20},{5,21},{6,22},{7,23},{8,24},{9,... | collective-permute-start | bytes 786440 | tf_op jit(solution)/shard_map/while/body/eval_jaxpr/ppermute | solution.py:12
  333.3 17.9 %copy-start.2 = (bf16[3,512,512]{2,1,0:T(8,128)(2,1)S(1)}, bf16[3,512,512]{2,1,0:T(8,128)(2,1)}, u32[]{:S(2)}) copy-start(bf16[3,512,512]{2,1,0:T(8,128)(2,1)} %get-tuple-element.414) | copy-start | bytes 4718596 | tf_op jit(solution)/shard_map/while
  335.3 9.9 %collective-permute-start.2 = (bf16[1,16,16,512]{3,2,1,0:T(8,128)(2,1)S(1)}, bf16[1,16,16,512]{3,2,1,0:T(8,128)(2,1)S(1)}, u32[]{:S(2)}, u32[]{:S(2)}) collective-permute-start(bf16[1,16,16,512]{3,2,1,0:T(8,128)(2,1)S(1)} %get-tuple-element.419), channel_id=1, source_target_pairs={{0,1},{1,2},{2,3},{3,4},{4,5},{5,6},{6,7},{7,8},{8,9},{9,10},{10,1... | collective-permute-start | bytes 786440 | tf_op jit(solution)/shard_map/while/body/eval_jaxpr/ppermute | solution.py:23
  343.9 7.4 %collective-permute-start.3 = (bf16[1,16,16,512]{3,2,1,0:T(8,128)(2,1)S(1)}, bf16[1,16,16,512]{3,2,1,0:T(8,128)(2,1)}, u32[]{:S(2)}, u32[]{:S(2)}) collective-permute-start(bf16[1,16,16,512]{3,2,1,0:T(8,128)(2,1)S(1)} %get-tuple-element.419), channel_id=1, source_target_pairs={{1,0},{2,1},{3,2},{4,3},{5,4},{6,5},{7,6},{8,7},{9,8},{10,9},{11,1... | collective-permute-start | bytes 786440 | tf_op jit(solution)/shard_map/while/body/eval_jaxpr/ppermute | solution.py:25
  (5 other events, 15.7 us)
Sparse Core Ops, SparseCore 0:
  9.6 55.8 all-gather.8
  67.7 38.1 all-gather.6
  108.1 51.6 all-gather.4
  354.5 65.8 all-reduce.3
